TPU v7x, 128 devices: a whole 4x4x4 slice. The times are simulated.
128 devices in a mesh: dst: 32 (over y, x, core), src: 4 (over z).
Axes of the slice: x: 4, y: 4, z: 4, core: 2. Of those that a mesh axis runs over, the one named last changes fastest.
Arguments:
- points: bfloat16 [16384, 256], P(('dst', 'src')), may hold values from -6 to 6
- w_query: bfloat16 [256, 256], replicated, may hold values from -16 to 16
- w_key: bfloat16 [256, 256], replicated, may hold values from -0.375 to 0.375
- w_value: bfloat16 [256, 256], replicated, may hold values from -0.375 to 0.375
- w_out: bfloat16 [256, 256], replicated, may hold values from -0.375 to 0.375
- gain: float32 [256], replicated, may hold values from 0.25 to 1.75
- cell_counts: int32 [32, 4], P('dst', 'src'), may hold values from 8 to 64, as said below
- tile_slots: int32 [32, 4, 64], P('dst', 'src'), may hold values from 0 to 127, as said below
- edge_masks: int32 [32, 4, 64, 128, 128], P('dst', 'src'), may hold values 0 or 1
Outputs:
- out_points: bfloat16 [16384, 256], P(('dst', 'src'))
Inputs may be any that keep to these rules, and one draw needn't show every extreme that they name: `cell_counts`: the busiest cell lists exactly 64 tiles. `tile_slots`: within one cell the 64 tile numbers are all different.
All inputs are finite; a program needn't handle non-finite values. No bound on the sum of `edge_masks` on one device may be relied on, other than what follows from the above.
Results may differ from a plain program's by a relative error of at most 0.0085.
The roundings to bfloat16 on the way count: a program that leaves them out, or rounds other values in their place, can miss the bound.
Values may be sent and summed in bfloat16 or wider, within the bound.
No kernel may reach another device: no remote copies, remote signals or barrier semaphores. Data moves between devices by JAX's collectives and lax.ppermute only.
A program may use at most 64 MiB of HBM per device.

v0:
```python
import math

import jax
import jax.numpy as jnp
from jax import lax
from jax.experimental import pallas as pl
from jax.experimental.pallas import tpu as pltpu
from jax.sharding import PartitionSpec as P


HEADS = 4
TILE = 128
PAIR = 2 * TILE
VROWS = TILE + 16
MASKED = -1e30
FLOOR = -1e29
PREP = 8
GROUP = 8
UNROLL = 4
F32 = jnp.float32
BF16 = jnp.bfloat16
VM = pltpu.VMEM
SM = pltpu.SMEM


def inverse_sinh(ratio):
    return jnp.log(ratio + jnp.sqrt(ratio * ratio + 1.0))


def log_map(points):
    values_f = points.astype(F32)
    radius = jnp.sqrt(jnp.sum(values_f * values_f, axis=-1, keepdims=True) + 1e-06)
    root_width = math.sqrt(points.shape[-1])
    return (root_width * inverse_sinh(radius / root_width) * values_f / radius).astype(BF16)


def gray(delta):
    return delta ^ (delta >> 1)


def prep_kernel(meta, slots, mask_ref, bias_ref, spot_out, group_out, pair_out, count_out, open_ref):
    step = pl.program_id(0)
    me_dst, me_src, live = meta[0], meta[1], meta[2]
    spare = slots.shape[0]
    trash = spare // 2 + 4 + UNROLL

    @pl.when(step == 0)
    def _():
        count_out[0] = 0
        for group in range(4):
            open_ref[group] = -1
        spot_out[spare] = 0

    opened = [open_ref[group] for group in range(4)]
    count = count_out[0]
    for member in range(PREP):
        slot = step * PREP + member
        named = slots[slot]
        group = gray((named >> 5) ^ me_src)
        delta = (named & 31) ^ me_dst
        spot_out[slot] = (delta & 1) * 16 + gray((delta >> 3) & 3) * 4 + gray((delta >> 1) & 3)
        group_out[slot] = group
        is_live = slot < live
        was_open = opened[3]
        for other in range(3):
            was_open = jnp.where(group == other, opened[other], was_open)
        is_fresh = was_open < 0
        fresh = is_fresh.astype(jnp.int32)
        pair = jnp.where(is_live, jnp.where(is_fresh, count, was_open), trash)
        count = count + jnp.where(is_live, fresh, 0)
        after = jnp.where(is_fresh, pair, -1)
        for other in range(4):
            opened[other] = jnp.where(is_live & (group == other), after, opened[other])
        pair_out[pair * 2 + 1] = spare
        pair_out[pair * 2 + 1 - fresh] = slot
        wanted = jnp.where(is_live, 1, 2)
        bias_ref[member] = jnp.where(mask_ref[member] == wanted, 0.0, MASKED).astype(BF16)
    count_out[0] = count
    for group in range(4):
        open_ref[group] = opened[group]

    @pl.when(step == pl.num_programs(0) - 1)
    def _():
        count = count_out[0]
        for extra in range(2 * UNROLL):
            pair_out[count * 2 + extra] = spare
        group_out[spare] = 0


def prepare(meta, slots, masks):
    tiles = masks.shape[0]
    sm = pl.BlockSpec(memory_space=SM)
    return pl.pallas_call(
        prep_kernel,
        grid=(tiles // PREP,),
        in_specs=[sm, sm, pl.BlockSpec((PREP, TILE, TILE), lambda i: (i, 0, 0))],
        out_specs=[pl.BlockSpec((PREP, TILE, TILE), lambda i: (i, 0, 0)), sm, sm, sm, sm],
        out_shape=[
            jax.ShapeDtypeStruct((tiles, TILE, TILE), BF16),
            jax.ShapeDtypeStruct((tiles + 8,), jnp.int32),
            jax.ShapeDtypeStruct((tiles + 8,), jnp.int32),
            jax.ShapeDtypeStruct((tiles + 10 + 2 * UNROLL,), jnp.int32),
            jax.ShapeDtypeStruct((1,), jnp.int32),
        ],
        scratch_shapes=[SM((4,), jnp.int32)],
        compiler_params=pltpu.CompilerParams(vmem_limit_bytes=8 << 20),
        cost_estimate=pl.CostEstimate(flops=1 << 20, bytes_accessed=6 << 20, transcendentals=0),
        name="prep",
    )(meta, slots, masks)


def nt_dot(left, right):
    return lax.dot_general(left, right, (((1,), (1,)), ((), ())), preferred_element_type=F32)


def project_rows(first_ref, second_ref, wk, wv, key_ref, value_ref, base):
    ones = jnp.ones((VROWS - TILE, TILE), BF16)

    @pl.loop(0, 4)
    def _(step):
        rows = []
        for member in range(4):
            rows.append(first_ref[pl.ds(pl.multiple_of((step * 4 + member) * 64, 64), 64), :])
            rows.append(second_ref[pl.ds(pl.multiple_of((member * 4 + step) * 64, 64), 64), :])
        rows = jnp.concatenate(rows, axis=0)
        keys = jnp.dot(rows, wk, preferred_element_type=F32).astype(BF16)
        values = nt_dot(wv, rows).astype(BF16)
        for member in range(4):
            at = base + step * 4 + member
            span = slice(member * TILE, (member + 1) * TILE)
            key_ref[at] = keys[span]
            for half in range(2):
                value_ref[at, half, pl.ds(0, TILE), :] = values[half * TILE : (half + 1) * TILE, span]
                value_ref[at, half, pl.ds(TILE, VROWS - TILE), :] = ones


def project_kernel(
    first_ref, second_ref, block_ref, wq_ref, wk_ref, wv_ref, key_ref, value_ref, query_ref, turned_ref, own_ref, self_ref
):
    wq, wk = wq_ref[...], wk_ref[...]
    wv_t = wv_ref[...].astype(F32).T.astype(BF16)
    turned_ref[...] = wv_t
    lane = lax.broadcasted_iota(jnp.int32, (TILE, TILE), 1)
    for group in range(4):
        rows = jnp.dot(block_ref[group], wq, preferred_element_type=F32).astype(BF16).astype(F32) * 0.125
        for half in range(2):
            part = rows[:, half * TILE : (half + 1) * TILE]
            query_ref[group, half, pl.ds(0, TILE), :] = jnp.where(lane < 64, part, 0.0).astype(BF16)
            query_ref[group, half, pl.ds(TILE, TILE), :] = jnp.where(lane < 64, 0.0, part).astype(BF16)
        if group == 0:
            own_keys = jnp.dot(block_ref[0], wk, preferred_element_type=F32).astype(BF16).astype(F32)
            product = (rows * own_keys).T
            for head in range(HEADS):
                total = jnp.sum(product[head * 64 : (head + 1) * 64], axis=0, keepdims=True)
                self_ref[pl.ds(head, 1), :] = total
            own_ref[...] = nt_dot(wv_t, block_ref[0]).astype(BF16)
    project_rows(first_ref, second_ref, wk, wv_t, key_ref, value_ref, 0)


def project(first, second, block, w_query, w_key, w_value):
    vm = pl.BlockSpec(memory_space=VM)
    return pl.pallas_call(
        project_kernel,
        in_specs=[vm] * 6,
        out_specs=[vm] * 6,
        out_shape=[
            jax.ShapeDtypeStruct((16, TILE, 256), BF16),
            jax.ShapeDtypeStruct((16, 2, VROWS, TILE), BF16),
            jax.ShapeDtypeStruct((4, 2, PAIR, TILE), BF16),
            jax.ShapeDtypeStruct((256, 256), BF16),
            jax.ShapeDtypeStruct((256, TILE), BF16),
            jax.ShapeDtypeStruct((HEADS, TILE), F32),
        ],
        compiler_params=pltpu.CompilerParams(vmem_limit_bytes=8 << 20),
        cost_estimate=pl.CostEstimate(flops=1 << 29, bytes_accessed=4 << 20, transcendentals=0),
        name="project",
    )(first, second, block, w_query, w_key, w_value)


def attend_kernel(
    meta, spot_list, group_list, pair_list, counts, bias_hbm, key_hbm, value_hbm, query_ref, first_ref, second_ref,
    wk_ref, wv_ref, part_ref, bias_ref, key_ref, value_ref, top_ref, acc_ref, score_ref, sem,
):
    tiles = bias_hbm.shape[0]
    copies = [
        pltpu.make_async_copy(bias_hbm, bias_ref, sem.at[0]),
        pltpu.make_async_copy(key_hbm, key_ref.at[pl.ds(0, 16)], sem.at[1]),
        pltpu.make_async_copy(value_hbm, value_ref.at[pl.ds(0, 16)], sem.at[2]),
    ]
    for copy in copies:
        copy.start()
    score_ref[tiles] = jnp.full((2, TILE, PAIR), MASKED, F32)
    top_ref[...] = jnp.full(top_ref.shape, FLOOR, F32)
    acc_ref[...] = jnp.zeros(acc_ref.shape, F32)
    project_rows(first_ref, second_ref, wk_ref[...], wv_ref[...], key_ref, value_ref, 16)
    for copy in copies:
        copy.wait()
    row = lax.broadcasted_iota(jnp.int32, (TILE, TILE), 0)
    lane = lax.broadcasted_iota(jnp.int32, (TILE, TILE), 1)
    eye = jnp.where(row == lane, 1.0, 0.0).astype(BF16)

    def score_step(trip, _):
        for member in range(GROUP):
            tile = trip * GROUP + member
            spot = spot_list[tile]
            group = group_list[tile]
            bias = bias_ref[tile]
            bias = jnp.concatenate([bias, bias], axis=0)
            for half in range(2):
                keys = jnp.concatenate([key_ref[spot, :, half * TILE : (half + 1) * TILE], eye], axis=1)
                queries = jnp.concatenate([query_ref[group, half], bias], axis=1)
                scores = nt_dot(keys, queries)
                score_ref[tile, half] = scores
                top = jnp.max(scores.reshape(16, 8, PAIR), axis=0)
                top_ref[group, half] = jnp.maximum(top_ref[group, half], top)
        return 0

    lax.fori_loop(0, (meta[2] + GROUP - 1) // GROUP, score_step, 0)
    for group in range(4):
        for half in range(2):
            top = jnp.max(top_ref[group, half], axis=0, keepdims=True)
            top_ref[group, half] = jnp.broadcast_to(top, (8, PAIR))

    def mix_step(trip, _):
        for member in range(UNROLL):
            pair = trip * UNROLL + member
            first, second = pair_list[pair * 2], pair_list[pair * 2 + 1]
            group = group_list[first]
            near, far = spot_list[first], spot_list[second]
            for half in range(2):
                top = top_ref[group, half, pl.ds(0, 1), :]
                weights = jnp.concatenate(
                    [jnp.exp(score_ref[tile, half] - top).astype(BF16) for tile in (first, second)], axis=0
                )
                values = jnp.concatenate([value_ref[near, half], value_ref[far, half]], axis=1)
                acc_ref[group, half] += jnp.dot(values, weights, preferred_element_type=F32)
        return 0

    lax.fori_loop(0, (counts[0] + UNROLL - 1) // UNROLL, mix_step, 0)
    for group in range(4):
        target = gray(group) ^ meta[1]
        for half in range(2):
            acc = acc_ref[group, half]
            part_ref[target, pl.ds(half * TILE, 64), :] = acc[:64, :TILE].astype(BF16)
            part_ref[target, pl.ds(half * TILE + 64, 64), :] = acc[64:TILE, TILE:].astype(BF16)
        rows = []
        for head in range(HEADS):
            half, lanes = head // 2, slice((head % 2) * TILE, (head % 2 + 1) * TILE)
            rows.append(top_ref[group, half, pl.ds(0, 1), lanes])
        for head in range(HEADS):
            half, lanes = head // 2, slice((head % 2) * TILE, (head % 2 + 1) * TILE)
            rows.append(acc_ref[group, half, pl.ds(TILE, 1), lanes])
        rest = jnp.concatenate(rows, axis=0)
        pieces = []
        for _ in range(4):
            piece = rest.astype(BF16)
            pieces.append(piece)
            rest = rest - piece.astype(F32)
        part_ref[target, pl.ds(256, 32), :] = jnp.concatenate(pieces, axis=0)


def attend(meta, lists, bias, keys, values, queries, first, second, w_key, wv_t):
    tiles = bias.shape[0]
    vm = pl.BlockSpec(memory_space=VM)
    sm = pl.BlockSpec(memory_space=SM)
    anywhere = pl.BlockSpec(memory_space=pl.ANY)
    return pl.pallas_call(
        attend_kernel,
        in_specs=[sm] * 5 + [anywhere] * 3 + [vm] * 5,
        out_specs=vm,
        out_shape=jax.ShapeDtypeStruct((4, 288, TILE), BF16),
        scratch_shapes=[
            VM((tiles, TILE, TILE), BF16),
            VM((32, TILE, 256), BF16),
            VM((32, 2, VROWS, TILE), BF16),
            VM((4, 2, 8, PAIR), F32),
            VM((4, 2, VROWS, PAIR), F32),
            VM((tiles + 1, 2, TILE, PAIR), F32),
            pltpu.SemaphoreType.DMA((3,)),
        ],
        compiler_params=pltpu.CompilerParams(vmem_limit_bytes=34 << 20),
        cost_estimate=pl.CostEstimate(flops=4 << 30, bytes_accessed=8 << 20, transcendentals=4 << 20),
        name="attend",
    )(meta, *lists, bias, keys, values, queries, first, second, w_key, wv_t)


def finish_kernel(part_ref, tangent_ref, own_ref, self_ref, wo_ref, gain_ref, out_ref):
    tangent = tangent_ref[...]
    vt = own_ref[...].astype(F32)
    stats = []
    for cell in range(4):
        pieces = part_ref[cell, pl.ds(256, 32), :].astype(F32)
        stats.append(pieces[:8] + pieces[8:16] + pieces[16:24] + pieces[24:])
    mixed = []
    for head in range(HEADS):
        rows = slice(head * 64, head * 64 + 64)
        own = self_ref[pl.ds(head, 1), :]
        tops = [stat[head : head + 1] for stat in stats]
        top = own
        for other in tops:
            top = jnp.maximum(top, other)
        own_exp = jnp.exp(own - top)
        total = own_exp
        weighted = own_exp.astype(BF16).astype(F32) * vt[rows]
        for cell in range(4):
            factor = jnp.exp(tops[cell] - top)
            total += stats[cell][4 + head : 5 + head] * factor
            weighted += part_ref[cell, pl.ds(head * 64, 64), :].astype(F32) * factor
        mixed.append((weighted / total).astype(BF16))
    mixed = jnp.concatenate(mixed, axis=0)
    shifted = tangent.astype(F32) + lax.dot_general(
        mixed, wo_ref[...], (((0,), (0,)), ((), ())), preferred_element_type=F32
    )
    normed = shifted / jnp.sqrt(jnp.mean(shifted * shifted, axis=-1, keepdims=True) + 1e-06) * gain_ref[...]
    radius = jnp.sqrt(jnp.sum(normed * normed, axis=-1, keepdims=True) + 1e-06)
    ratio = radius / 16.0
    square = ratio * ratio
    series = ratio * (
        1.0 + square / 6.0 * (1.0 + square / 20.0 * (1.0 + square / 42.0 * (1.0 + square / 72.0)))
    )
    plain = 0.5 * (jnp.exp(ratio) - jnp.exp(-ratio))
    stretched = jnp.where(ratio < 0.75, series, plain)
    out_ref[...] = (16.0 * stretched * normed / radius).astype(BF16)


def finish(part, tangent, own, self_score, w_out, gain):
    vm = pl.BlockSpec(memory_space=VM)
    return pl.pallas_call(
        finish_kernel,
        in_specs=[vm] * 6,
        out_specs=vm,
        out_shape=jax.ShapeDtypeStruct(tangent.shape, BF16),
        compiler_params=pltpu.CompilerParams(vmem_limit_bytes=8 << 20),
        cost_estimate=pl.CostEstimate(flops=1 << 26, bytes_accessed=1 << 20, transcendentals=1 << 12),
        name="finish",
    )(part, tangent, own, self_score, w_out, gain)


def swap(value, axis, size, mask):
    return lax.ppermute(value, axis, [(at, at ^ mask) for at in range(size)])


def grow(value, axis, size, mask):
    return jnp.concatenate([value, swap(value, axis, size, mask)], axis=0)


def per_device(points, w_query, w_key, w_value, w_out, gain, cell_counts, tile_slots, edge_masks):
    me_dst = lax.axis_index("dst")
    me_src = lax.axis_index("src")
    meta = jnp.stack([me_dst, me_src, cell_counts[0, 0]]).astype(jnp.int32)
    tangent = log_map(points)
    first, second, block = tangent[:64], tangent[64:], tangent
    for hop, (one, other) in enumerate(((2, 8), (6, 24), (8, 2), (24, 6))):
        new_first = grow(first, "dst", 32, one)
        second = grow(second, "dst", 32, other)
        first = new_first
        if hop < 2:
            block = grow(block, "src", 4, (1, 3)[hop])
            first, second, block = lax.optimization_barrier((first, second, block))
    far_first = swap(first, "dst", 32, 1)
    far_second = swap(second, "dst", 32, 1)
    bias, *lists = prepare(meta, tile_slots[0, 0], edge_masks[0, 0])
    keys, values, queries, wv_t, own, self_score = project(
        first, second, block.reshape(4, TILE, 256), w_query, w_key, w_value
    )
    part = attend(meta, lists, bias, keys, values, queries, far_first, far_second, w_key, wv_t)
    part = lax.all_to_all(part, "src", 0, 0)
    return finish(part, tangent, own, self_score, w_out, gain[None, :])


def solution(mesh):
    return jax.shard_map(
        per_device,
        mesh=mesh,
        in_specs=(
            P(("dst", "src"), None),
            P(),
            P(),
            P(),
            P(),
            P(),
            P("dst", "src"),
            P("dst", "src", None),
            P("dst", "src", None, None, None),
        ),
        out_specs=P(("dst", "src"), None),
        check_vma=False,
    )
```

profile of v0, /device:TPU:1, one launch (start us, length us, event | category | flops | bytes accessed | tf_op | source)
XLA Modules:
  0.0 68.1 jit_solution(17516727499802512007)
XLA Ops:
  0.0 0.9 %fusion = f32[128]{0:T(128)S(1)} fusion(bf16[128,256]{1,0:T(8,128)(2,1)} %param.9), kind=kLoop, calls=%fused_computation.5 | loop fusion | flops 98176 | bytes 66048 | tf_op jit(solution)/shard_map/reduce_sum | solution.py:32
  1.0 1.0 %fusion.2.tangent_ref = bf16[128,256]{1,0:T(8,128)(2,1)S(1)} fusion(bf16[128,256]{1,0:T(8,128)(2,1)} %param.9, f32[128]{0:T(128)S(1)} %get-tuple-element.42, f32[128]{0:T(128)S(1)} %get-tuple-element.41), kind=kLoop, calls=%fused_computation.7 | loop fusion | flops 131072 | bytes 132096 | tf_op jit(solution)/shard_map/convert_element_type | solution.py:34
  2.0 2.1 %collective-permute-start = (bf16[64,256]{1,0:T(8,128)(2,1)S(1)}, bf16[64,256]{1,0:T(8,128)(2,1)S(1)}, u32[]{:S(2)}, u32[]{:S(2)}) collective-permute-start(bf16[64,256]{1,0:T(8,128)(2,1)S(1)} %get-tuple-element.40), channel_id=1, source_target_pairs={{0,8},{4,12},{8,0},{12,4},{16,24},{20,28},{24,16},{28,20},{32,40},... | collective-permute-start | bytes 98312 | tf_op jit(solution)/shard_map/ppermute | solution.py:340
  4.1 1.6 %collective-permute-start.2 = (bf16[128,256]{1,0:T(8,128)(2,1)S(1)}, bf16[128,256]{1,0:T(8,128)(2,1)S(1)}, u32[]{:S(2)}, u32[]{:S(2)}) collective-permute-start(bf16[128,256]{1,0:T(8,128)(2,1)S(1)} %fusion.2.tangent_ref), channel_id=1, source_target_pairs={{0,1},{1,0},{2,3},{3,2},{4,5},{5,4},{6,7},{7,6},{8,9},{9,8},{10,11... | collective-permute-start | bytes 196616 | tf_op jit(solution)/shard_map/ppermute | solution.py:340
  5.7 1.3 %collective-permute-start.1 = (bf16[64,256]{1,0:T(8,128)(2,1)S(1)}, bf16[64,256]{1,0:T(8,128)(2,1)S(1)}, u32[]{:S(2)}, u32[]{:S(2)}) collective-permute-start(bf16[64,256]{1,0:T(8,128)(2,1)S(1)} %get-tuple-element.39), channel_id=1, source_target_pairs={{0,32},{4,36},{8,40},{12,44},{16,48},{20,52},{24,56},{28,60},{32,0... | collective-permute-start | bytes 98312 | tf_op jit(solution)/shard_map/ppermute | solution.py:340
  7.0 0.0 collective-permute-done
  7.0 1.8 %collective-permute-done.1 = bf16[64,256]{1,0:T(8,128)(2,1)S(1)} collective-permute-done((bf16[64,256]{1,0:T(8,128)(2,1)S(1)}, bf16[64,256]{1,0:T(8,128)(2,1)S(1)}, u32[]{:S(2)}, u32[]{:S(2)}) %collective-permute-start.1) | collective-permute-done | bytes 32800 | tf_op jit(solution)/shard_map/ppermute | solution.py:340
  8.8 0.0 collective-permute-done.2
  8.8 0.0 copy-start.3
  8.8 1.9 %collective-permute-start.3 = (bf16[128,256]{1,0:T(8,128)(2,1)S(1)}, bf16[128,256]{1,0:T(8,128)(2,1)S(1)}, u32[]{:S(2)}, u32[]{:S(2)}) collective-permute-start(bf16[128,256]{1,0:T(8,128)(2,1)S(1)} %pad_maximum_fusion.6), channel_id=1, source_target_pairs={{0,24},{4,28},{8,16},{12,20},{16,8},{20,12},{24,0},{28,4},{32,56},... | collective-permute-start | bytes 196616 | tf_op jit(solution)/shard_map/ppermute | solution.py:340
  10.7 2.5 %collective-permute-start.5 = (bf16[256,256]{1,0:T(8,128)(2,1)S(1)}, bf16[256,256]{1,0:T(8,128)(2,1)S(1)}, u32[]{:S(2)}, u32[]{:S(2)}) collective-permute-start(bf16[256,256]{1,0:T(8,128)(2,1)S(1)} %pad_maximum_fusion.3), channel_id=1, source_target_pairs={{0,3},{1,2},{2,1},{3,0},{4,7},{5,6},{6,5},{7,4},{8,11},{9,10},{10,... | collective-permute-start | bytes 393224 | tf_op jit(solution)/shard_map/ppermute | solution.py:340
  13.2 2.7 %collective-permute-start.4 = (bf16[128,256]{1,0:T(8,128)(2,1)S(1)}, bf16[128,256]{1,0:T(8,128)(2,1)S(1)}, u32[]{:S(2)}, u32[]{:S(2)}) collective-permute-start(bf16[128,256]{1,0:T(8,128)(2,1)S(1)} %pad_maximum_fusion.7), channel_id=1, source_target_pairs={{0,96},{4,100},{8,104},{12,108},{16,112},{20,116},{24,120},{28,124... | collective-permute-start | bytes 196616 | tf_op jit(solution)/shard_map/ppermute | solution.py:340
  15.9 0.0 collective-permute-done.3
  15.9 1.9 %collective-permute-done.4 = bf16[128,256]{1,0:T(8,128)(2,1)S(1)} collective-permute-done((bf16[128,256]{1,0:T(8,128)(2,1)S(1)}, bf16[128,256]{1,0:T(8,128)(2,1)S(1)}, u32[]{:S(2)}, u32[]{:S(2)}) %collective-permute-start.4) | collective-permute-done | bytes 65568 | tf_op jit(solution)/shard_map/ppermute | solution.py:340
  17.8 0.0 collective-permute-done.5
  17.9 0.3 collective-permute-start.8
  18.1 0.0 collective-permute-start.6
  18.2 3.6 %collective-permute-done.8 = bf16[256,256]{1,0:T(8,128)(2,1)S(1)} collective-permute-done((bf16[256,256]{1,0:T(8,128)(2,1)S(1)}, bf16[256,256]{1,0:T(8,128)(2,1)S(1)}, u32[]{:S(2)}, u32[]{:S(2)}) %collective-permute-start.8) | collective-permute-done | bytes 131104 | tf_op jit(solution)/shard_map/ppermute | solution.py:340
  21.8 0.6 collective-permute-start.9
  22.5 0.0 collective-permute-done.6
  22.5 2.8 %collective-permute-start.7 = (bf16[512,256]{1,0:T(8,128)(2,1)S(1)}, bf16[512,256]{1,0:T(8,128)(2,1)S(1)}, u32[]{:S(2)}, u32[]{:S(2)}) collective-permute-start(bf16[512,256]{1,0:T(8,128)(2,1)S(1)} %pad_maximum_fusion.1), channel_id=1, source_target_pairs={{0,96},{4,100},{8,104},{12,108},{16,112},{20,116},{24,120},{28,124... | collective-permute-start | bytes 786440 | tf_op jit(solution)/shard_map/ppermute | solution.py:340
  25.3 3.1 %collective-permute-done.9 = bf16[512,256]{1,0:T(8,128)(2,1)S(1)} collective-permute-done((bf16[512,256]{1,0:T(8,128)(2,1)S(1)}, bf16[512,256]{1,0:T(8,128)(2,1)S(1)}, u32[]{:S(2)}, u32[]{:S(2)}) %collective-permute-start.9) | collective-permute-done | bytes 262176 | tf_op jit(solution)/shard_map/ppermute | solution.py:340
  28.3 5.6 %collective-permute-start.11 = (bf16[1024,256]{1,0:T(8,128)(2,1)S(1)}, bf16[1024,256]{1,0:T(8,128)(2,1)S(1)}, u32[]{:S(2)}, u32[]{:S(2)}) collective-permute-start(bf16[1024,256]{1,0:T(8,128)(2,1)S(1)} %constant_dynamic-update-slice_fusion.3.second_ref), channel_id=1, source_target_pairs={{0,4},{4,0},{8,12},{12,8},{16,20},{20,16},{24,28},{28,24},{32,36},... | collective-permute-start | bytes 1572872 | tf_op jit(solution)/shard_map/ppermute | solution.py:340
  34.0 0.0 collective-permute-done.7
  34.0 1.2 %collective-permute-start.10 = (bf16[1024,256]{1,0:T(8,128)(2,1)S(1)}, bf16[1024,256]{1,0:T(8,128)(2,1)S(1)}, u32[]{:S(2)}, u32[]{:S(2)}) collective-permute-start(bf16[1024,256]{1,0:T(8,128)(2,1)S(1)} %constant_dynamic-update-slice_fusion.first_ref), channel_id=1, source_target_pairs={{0,4},{4,0},{8,12},{12,8},{16,20},{20,16},{24,28},{28,24},{32,36},... | collective-permute-start | bytes 1572872 | tf_op jit(solution)/shard_map/ppermute | solution.py:340
  35.9 0.1 pad_add_fusion.meta
  35.9 0.0 copy-done.3
  35.9 0.0 copy-start
  35.9 2.2 %copy-done = s32[1,1,64,128,128]{4,3,2,1,0:T(8,128)S(1)} copy-done((s32[1,1,64,128,128]{4,3,2,1,0:T(8,128)S(1)}, s32[1,1,64,128,128]{4,3,2,1,0:T(8,128)}, u32[]{:S(2)}) %copy-start) | copy-done | bytes 4194328
  38.1 0.0 copy-start.4
  38.1 0.0 copy-start.5
  38.1 0.0 copy-start.6
  38.1 2.8 %prep.1 = (bf16[64,128,128]{2,1,0:T(8,128)(2,1)S(1)}, s32[72]{0:T(128)S(1)}, s32[72]{0:T(128)S(1)}, s32[82]{0:T(128)S(1)}, s32[1]{0:T(128)}) custom-call(s32[3]{0:T(128)S(1)} %pad_add_fusion.meta, s32[64]{0:T(128)S(1)} %bitcast.11, s32[64,128,128]{2,1,0:T(8,128)S(1)} %bitcast.8), custom_call_target="tpu_custom_call" | custom-call | flops 1048576 | bytes 6291456 | tf_op jit(solution)/shard_map/prep/pallas_call | solution.py:93
  40.9 0.0 copy-done.4
  40.9 0.0 copy-done.5
  40.9 0.0 copy-done.6
  40.9 1.6 %project.1 = (bf16[16,128,256]{2,1,0:T(8,128)(2,1)S(1)}, bf16[16,2,144,128]{3,2,1,0:T(8,128)(2,1)S(1)}, bf16[4,2,256,128]{3,2,1,0:T(8,128)(2,1)S(1)}, bf16[256,2...) custom-call(bf16[1024,256]{1,0:T(8,128)(2,1)S(1)} %constant_dynamic-update-slice_fusion.first_ref, ...), custom_call_target="tpu_custom_call" | custom-call | flops 536870912 | bytes 4194304 | tf_op jit(solution)/shard_map/project/pallas_call | solution.py:162
  42.5 0.0 collective-permute-done.11.second_ref
  42.5 0.0 collective-permute-done.10.first_ref
  42.5 0.0 copy-start.1
  42.5 0.0 copy-start.2
  42.6 14.6 %attend.1 = bf16[4,288,128]{2,1,0:T(8,128)(2,1)S(1)} custom-call(s32[3]{0:T(128)S(1)} %pad_add_fusion.meta, s32[72]{0:T(128)S(1)} %get-tuple-element.22.spot_list, s32[72]{0:T(128)S(1)} %get-tuple-element.23.group_list, s32[82]{0:T(128)S(1)} %get-tuple-element.24.pair_list, s32[1]{0:T(128)} %get-tuple-element.25.counts, ...), custom_call_target="tpu_custom_call" | custom-call | flops 4294967296 | bytes 8388608 | tf_op jit(solution)/shard_map/attend/pallas_call | solution.py:267
  57.2 9.7 %all_to_all.5.part_ref = bf16[4,288,128]{2,1,0:T(8,128)(2,1)S(1)} all-to-all(bf16[4,288,128]{2,1,0:T(8,128)(2,1)S(1)} %attend.1), channel_id=1, replica_groups=mesh['dst'=32,'src'=4] {'src'}, dimensions={0} | all-to-all | bytes 589824 | tf_op jit(solution)/shard_map/all_to_all | solution.py:367
  66.9 0.0 copy-done.1
  66.9 0.0 copy-done.2
  66.9 1.2 %finish.1 = bf16[128,256]{1,0:T(8,128)(2,1)} custom-call(bf16[4,288,128]{2,1,0:T(8,128)(2,1)S(1)} %all_to_all.5.part_ref, bf16[128,256]{1,0:T(8,128)(2,1)S(1)} %fusion.2.tangent_ref, bf16[256,128]{1,0:T(8,128)(2,1)S(1)} %get-tuple-element.37.own_ref, f32[4,128]{1,0:T(4,128)S(1)} %get-tuple-element.38.self_ref, bf16[256,256]{1,0:T(8,128)(2,1)S(1)} %copy-done.1, ...), custom_call_target="tpu_custom_call" | custom-call | flops 67108864 | bytes 1048576 | tf_op jit(solution)/shard_map/finish/pallas_call | solution.py:328
  (15 shorter events, 0.2 us)
Async XLA Ops:
  2.0 5.0 %collective-permute-start = (bf16[64,256]{1,0:T(8,128)(2,1)S(1)}, bf16[64,256]{1,0:T(8,128)(2,1)S(1)}, u32[]{:S(2)}, u32[]{:S(2)}) collective-permute-start(bf16[64,256]{1,0:T(8,128)(2,1)S(1)} %get-tuple-element.40), channel_id=1, source_target_pairs={{0,8},{4,12},{8,0},{12,4},{16,24},{20,28},{24,16},{28,20},{32,40},... | collective-permute-start | bytes 98312 | tf_op jit(solution)/shard_map/ppermute | solution.py:340
  4.1 4.7 %collective-permute-start.2 = (bf16[128,256]{1,0:T(8,128)(2,1)S(1)}, bf16[128,256]{1,0:T(8,128)(2,1)S(1)}, u32[]{:S(2)}, u32[]{:S(2)}) collective-permute-start(bf16[128,256]{1,0:T(8,128)(2,1)S(1)} %fusion.2.tangent_ref), channel_id=1, source_target_pairs={{0,1},{1,0},{2,3},{3,2},{4,5},{5,4},{6,7},{7,6},{8,9},{9,8},{10,11... | collective-permute-start | bytes 196616 | tf_op jit(solution)/shard_map/ppermute | solution.py:340
  5.7 3.1 %collective-permute-start.1 = (bf16[64,256]{1,0:T(8,128)(2,1)S(1)}, bf16[64,256]{1,0:T(8,128)(2,1)S(1)}, u32[]{:S(2)}, u32[]{:S(2)}) collective-permute-start(bf16[64,256]{1,0:T(8,128)(2,1)S(1)} %get-tuple-element.39), channel_id=1, source_target_pairs={{0,32},{4,36},{8,40},{12,44},{16,48},{20,52},{24,56},{28,60},{32,0... | collective-permute-start | bytes 98312 | tf_op jit(solution)/shard_map/ppermute | solution.py:340
  8.8 27.1 %copy-start.3 = (s32[1,1,64]{2,1,0:T(1,128)S(1)}, s32[1,1,64]{2,1,0:T(1,128)}, u32[]{:S(2)}) copy-start(s32[1,1,64]{2,1,0:T(1,128)} %param.16) | copy-start | bytes 772
  8.8 7.1 %collective-permute-start.3 = (bf16[128,256]{1,0:T(8,128)(2,1)S(1)}, bf16[128,256]{1,0:T(8,128)(2,1)S(1)}, u32[]{:S(2)}, u32[]{:S(2)}) collective-permute-start(bf16[128,256]{1,0:T(8,128)(2,1)S(1)} %pad_maximum_fusion.6), channel_id=1, source_target_pairs={{0,24},{4,28},{8,16},{12,20},{16,8},{20,12},{24,0},{28,4},{32,56},... | collective-permute-start | bytes 196616 | tf_op jit(solution)/shard_map/ppermute | solution.py:340
  10.7 7.2 %collective-permute-start.5 = (bf16[256,256]{1,0:T(8,128)(2,1)S(1)}, bf16[256,256]{1,0:T(8,128)(2,1)S(1)}, u32[]{:S(2)}, u32[]{:S(2)}) collective-permute-start(bf16[256,256]{1,0:T(8,128)(2,1)S(1)} %pad_maximum_fusion.3), channel_id=1, source_target_pairs={{0,3},{1,2},{2,1},{3,0},{4,7},{5,6},{6,5},{7,4},{8,11},{9,10},{10,... | collective-permute-start | bytes 393224 | tf_op jit(solution)/shard_map/ppermute | solution.py:340
  13.2 4.7 %collective-permute-start.4 = (bf16[128,256]{1,0:T(8,128)(2,1)S(1)}, bf16[128,256]{1,0:T(8,128)(2,1)S(1)}, u32[]{:S(2)}, u32[]{:S(2)}) collective-permute-start(bf16[128,256]{1,0:T(8,128)(2,1)S(1)} %pad_maximum_fusion.7), channel_id=1, source_target_pairs={{0,96},{4,100},{8,104},{12,108},{16,112},{20,116},{24,120},{28,124... | collective-permute-start | bytes 196616 | tf_op jit(solution)/shard_map/ppermute | solution.py:340
  17.9 3.9 %collective-permute-start.8 = (bf16[256,256]{1,0:T(8,128)(2,1)S(1)}, bf16[256,256]{1,0:T(8,128)(2,1)S(1)}, u32[]{:S(2)}, u32[]{:S(2)}) collective-permute-start(bf16[256,256]{1,0:T(8,128)(2,1)S(1)} %pad_maximum_fusion.5), channel_id=1, source_target_pairs={{0,8},{4,12},{8,0},{12,4},{16,24},{20,28},{24,16},{28,20},{32,40},... | collective-permute-start | bytes 393224 | tf_op jit(solution)/shard_map/ppermute | solution.py:340
  18.1 4.3 %collective-permute-start.6 = (bf16[256,256]{1,0:T(8,128)(2,1)S(1)}, bf16[256,256]{1,0:T(8,128)(2,1)S(1)}, u32[]{:S(2)}, u32[]{:S(2)}) collective-permute-start(bf16[256,256]{1,0:T(8,128)(2,1)S(1)} %pad_maximum_fusion.4), channel_id=1, source_target_pairs={{0,32},{4,36},{8,40},{12,44},{16,48},{20,52},{24,56},{28,60},{32,0... | collective-permute-start | bytes 393224 | tf_op jit(solution)/shard_map/ppermute | solution.py:340
  21.8 6.5 %collective-permute-start.9 = (bf16[512,256]{1,0:T(8,128)(2,1)S(1)}, bf16[512,256]{1,0:T(8,128)(2,1)S(1)}, u32[]{:S(2)}, u32[]{:S(2)}) collective-permute-start(bf16[512,256]{1,0:T(8,128)(2,1)S(1)} %pad_maximum_fusion.2), channel_id=1, source_target_pairs={{0,24},{4,28},{8,16},{12,20},{16,8},{20,12},{24,0},{28,4},{32,56},... | collective-permute-start | bytes 786440 | tf_op jit(solution)/shard_map/ppermute | solution.py:340
  22.5 11.5 %collective-permute-start.7 = (bf16[512,256]{1,0:T(8,128)(2,1)S(1)}, bf16[512,256]{1,0:T(8,128)(2,1)S(1)}, u32[]{:S(2)}, u32[]{:S(2)}) collective-permute-start(bf16[512,256]{1,0:T(8,128)(2,1)S(1)} %pad_maximum_fusion.1), channel_id=1, source_target_pairs={{0,96},{4,100},{8,104},{12,108},{16,112},{20,116},{24,120},{28,124... | collective-permute-start | bytes 786440 | tf_op jit(solution)/shard_map/ppermute | solution.py:340
  28.3 14.2 %collective-permute-start.11 = (bf16[1024,256]{1,0:T(8,128)(2,1)S(1)}, bf16[1024,256]{1,0:T(8,128)(2,1)S(1)}, u32[]{:S(2)}, u32[]{:S(2)}) collective-permute-start(bf16[1024,256]{1,0:T(8,128)(2,1)S(1)} %constant_dynamic-update-slice_fusion.3.second_ref), channel_id=1, source_target_pairs={{0,4},{4,0},{8,12},{12,8},{16,20},{20,16},{24,28},{28,24},{32,36},... | collective-permute-start | bytes 1572872 | tf_op jit(solution)/shard_map/ppermute | solution.py:340
  34.0 8.5 %collective-permute-start.10 = (bf16[1024,256]{1,0:T(8,128)(2,1)S(1)}, bf16[1024,256]{1,0:T(8,128)(2,1)S(1)}, u32[]{:S(2)}, u32[]{:S(2)}) collective-permute-start(bf16[1024,256]{1,0:T(8,128)(2,1)S(1)} %constant_dynamic-update-slice_fusion.first_ref), channel_id=1, source_target_pairs={{0,4},{4,0},{8,12},{12,8},{16,20},{20,16},{24,28},{28,24},{32,36},... | collective-permute-start | bytes 1572872 | tf_op jit(solution)/shard_map/ppermute | solution.py:340
  35.9 2.2 %copy-start = (s32[1,1,64,128,128]{4,3,2,1,0:T(8,128)S(1)}, s32[1,1,64,128,128]{4,3,2,1,0:T(8,128)}, u32[]{:S(2)}) copy-start(s32[1,1,64,128,128]{4,3,2,1,0:T(8,128)} %param.17) | copy-start | bytes 12582916
  38.1 2.8 %copy-start.4 = (bf16[256,256]{1,0:T(8,128)(2,1)S(1)}, bf16[256,256]{1,0:T(8,128)(2,1)}, u32[]{:S(2)}) copy-start(bf16[256,256]{1,0:T(8,128)(2,1)} %wq_ref.1) | copy-start | bytes 393220
  38.1 2.8 %copy-start.5 = (bf16[256,256]{1,0:T(8,128)(2,1)S(1)}, bf16[256,256]{1,0:T(8,128)(2,1)}, u32[]{:S(2)}) copy-start(bf16[256,256]{1,0:T(8,128)(2,1)} %wv_ref.1) | copy-start | bytes 393220
  38.1 2.8 %copy-start.6 = (bf16[256,256]{1,0:T(8,128)(2,1)S(1)}, bf16[256,256]{1,0:T(8,128)(2,1)}, u32[]{:S(2)}) copy-start(bf16[256,256]{1,0:T(8,128)(2,1)} %wk_ref.3) | copy-start | bytes 393220
  42.5 24.4 %copy-start.1 = (bf16[256,256]{1,0:T(8,128)(2,1)S(1)}, bf16[256,256]{1,0:T(8,128)(2,1)}, u32[]{:S(2)}) copy-start(bf16[256,256]{1,0:T(8,128)(2,1)} %wo_ref.1) | copy-start | bytes 393220
  42.5 24.4 %copy-start.2 = (f32[256]{0:T(256)S(1)}, f32[256]{0:T(256)}, u32[]{:S(2)}) copy-start(f32[256]{0:T(256)} %param.14) | copy-start | bytes 3076
where the time goes:
time: 68.4 us; the launch traced here: 68.1 us
  starting transfers between devices  22.6 us (33%)
  Pallas kernels  20.1 us (29%)
  waiting for transfers between devices  10.4 us (15%)
  blocking collectives  9.75 us (14%)
  local copies, waits for them, and re-layouts  2.3 us (3%)
  other arithmetic  2.09 us (3%)
  between operations  0.85 us (1%)
    ppermute x12, starting transfers between devices, swap(): return lax.ppermute(value, axis, [(at, at ^ mask) for at in range(size)])  22.6 us
    pallas_call x1, Pallas kernels, attend(): pl.pallas_call(attend_kernel, in_specs=[sm] * 5 + [anywhere] * 3 + [vm] *...  14.6 us
    ppermute x12, waiting for transfers between devices, swap(): return lax.ppermute(value, axis, [(at, at ^ mask) for at in range(size)])  10.4 us
    all_to_all x1, blocking collectives, per_device(): part = lax.all_to_all(part, 'src', 0, 0)  9.75 us
    pallas_call x1, Pallas kernels, prepare(): pl.pallas_call(prep_kernel, grid=(tiles // PREP,), in_specs=[sm, sm, pl.B...  2.78 us
    unnamed x17, local copies, waits for them, and re-layouts  2.26 us
    pallas_call x1, Pallas kernels, project(): pl.pallas_call(project_kernel, in_specs=[vm] * 6, out_specs=[vm] * 6, out...  1.55 us
  transfers between devices with their start and end apart: 12, of which 4 were waited for; matrix products, arithmetic and copies ran while one was open for 0% of the time, Pallas kernels for 6%

commit v1 on v0

v1 whole, which is shorter than its diff:
```python
import functools
import math

import jax
import jax.numpy as jnp
from jax import lax
from jax.experimental import pallas as pl
from jax.experimental.pallas import tpu as pltpu
from jax.sharding import PartitionSpec as P


HEADS = 4
TILE = 128
PAIR = 2 * TILE
VROWS = TILE + 16
MASKED = -1e30
FLOOR = -1e29
PREP = 8
QUAD = 4
STRIDE = 40
F32 = jnp.float32
BF16 = jnp.bfloat16
VM = pltpu.VMEM
SM = pltpu.SMEM


def inverse_sinh(ratio):
    return jnp.log(ratio + jnp.sqrt(ratio * ratio + 1.0))


def log_map(points):
    values_f = points.astype(F32)
    radius = jnp.sqrt(jnp.sum(values_f * values_f, axis=-1, keepdims=True) + 1e-06)
    root_width = math.sqrt(points.shape[-1])
    return (root_width * inverse_sinh(radius / root_width) * values_f / radius).astype(BF16)


def gray(delta):
    return delta ^ (delta >> 1)


def prep_kernel(meta, slots, mask_hbm, bias_ref, spot_out, tile_out, count_out, mask_ref, sem):
    me_dst, me_src, live = meta[0], meta[1], meta[2]
    spare = slots.shape[0]

    def fetch(trip):
        span = pl.ds(trip * PREP, PREP)
        return pltpu.make_async_copy(mask_hbm.at[span], mask_ref.at[span], sem.at[trip])

    for trip in range(spare // PREP):
        fetch(trip).start()
    row = lax.broadcasted_iota(jnp.int32, (TILE, TILE), 0)
    lane = lax.broadcasted_iota(jnp.int32, (TILE, TILE), 1)
    eye = jnp.where(row == lane, 1.0, 0.0).astype(BF16)
    bias_ref[spare] = jnp.full((TILE, TILE), MASKED, BF16)
    spot_out[spare] = 0

    def step(trip, counts):
        counts = list(counts)
        fetch(trip).wait()
        for member in range(PREP):
            slot = trip * PREP + member
            named = slots[slot]
            group = gray((named >> 5) ^ me_src)
            delta = (named & 31) ^ me_dst
            spot_out[slot] = (delta & 1) * 16 + gray((delta >> 3) & 3) * 4 + gray((delta >> 1) & 3)
            at = counts[3]
            for other in range(3):
                at = jnp.where(group == other, counts[other], at)
            is_live = slot < live
            tile_out[jnp.where(is_live, group * STRIDE + at, 4 * STRIDE)] = slot
            for other in range(4):
                counts[other] = counts[other] + (is_live & (group == other)).astype(jnp.int32)
            wanted = jnp.where(is_live, 1, 2)
            bias = jnp.where(mask_ref[slot] == wanted, 0.0, MASKED).astype(BF16)
            bias_ref[slot] = nt_dot(eye, bias).astype(BF16)
        return tuple(counts)

    zero = jnp.int32(0)
    counts = lax.fori_loop(0, spare // PREP, step, (zero,) * 4)
    for group in range(4):
        count_out[group] = counts[group]
        for extra in range(QUAD):
            tile_out[group * STRIDE + counts[group] + extra] = spare


def prepare(meta, slots, masks):
    tiles = masks.shape[0]
    vm = pl.BlockSpec(memory_space=VM)
    sm = pl.BlockSpec(memory_space=SM)
    return pl.pallas_call(
        prep_kernel,
        in_specs=[sm, sm, pl.BlockSpec(memory_space=pltpu.HBM)],
        out_specs=[vm, sm, sm, sm],
        out_shape=[
            jax.ShapeDtypeStruct((tiles + 1, TILE, TILE), BF16),
            jax.ShapeDtypeStruct((tiles + 8,), jnp.int32),
            jax.ShapeDtypeStruct((4 * STRIDE + 8,), jnp.int32),
            jax.ShapeDtypeStruct((4,), jnp.int32),
        ],
        scratch_shapes=[VM(masks.shape, jnp.int32), pltpu.SemaphoreType.DMA((tiles // PREP,))],
        compiler_params=pltpu.CompilerParams(vmem_limit_bytes=8 << 20),
        cost_estimate=pl.CostEstimate(flops=1 << 20, bytes_accessed=6 << 20, transcendentals=0),
        name="prep",
    )(meta, slots, masks)


def nt_dot(left, right):
    return lax.dot_general(left, right, (((1,), (1,)), ((), ())), preferred_element_type=F32)


def project_rows(first_ref, second_ref, wk, wv, key_ref, value_ref, base):
    ones = jnp.ones((VROWS - TILE, TILE), BF16)

    @pl.loop(0, 4)
    def _(step):
        rows = []
        for member in range(4):
            rows.append(first_ref[pl.ds(pl.multiple_of((step * 4 + member) * 64, 64), 64), :])
            rows.append(second_ref[pl.ds(pl.multiple_of((member * 4 + step) * 64, 64), 64), :])
        rows = jnp.concatenate(rows, axis=0)
        keys = jnp.dot(rows, wk, preferred_element_type=F32).astype(BF16)
        values = nt_dot(wv, rows).astype(BF16)
        for member in range(4):
            at = base + step * 4 + member
            span = slice(member * TILE, (member + 1) * TILE)
            key_ref[at] = keys[span]
            for half in range(2):
                value_ref[at, half, pl.ds(0, TILE), :] = values[half * TILE : (half + 1) * TILE, span]
                value_ref[at, half, pl.ds(TILE, VROWS - TILE), :] = ones


def project_kernel(
    first_ref, second_ref, block_ref, wq_ref, wk_ref, wv_ref, key_ref, value_ref, query_ref, turned_ref, own_ref, self_ref
):
    wq, wk = wq_ref[...], wk_ref[...]
    wv_t = wv_ref[...].astype(F32).T.astype(BF16)
    turned_ref[...] = wv_t
    wq_t = wq.astype(F32).T.astype(BF16)
    zero = jnp.zeros((64, TILE), BF16)
    for group in range(4):
        qt = nt_dot(wq_t, block_ref[group]).astype(BF16).astype(F32) * 0.125
        low = qt.astype(BF16)
        for half in range(2):
            upper = jnp.concatenate([low[half * TILE : half * TILE + 64], zero], axis=1)
            lower = jnp.concatenate([zero, low[half * TILE + 64 : half * TILE + TILE]], axis=1)
            query_ref[group, half] = jnp.concatenate([upper, lower], axis=0)
        if group == 0:
            wk_t = wk.astype(F32).T.astype(BF16)
            product = qt * nt_dot(wk_t, block_ref[0]).astype(BF16).astype(F32)
            for head in range(HEADS):
                total = jnp.sum(product[head * 64 : (head + 1) * 64], axis=0, keepdims=True)
                self_ref[pl.ds(head, 1), :] = total
            own_ref[...] = nt_dot(wv_t, block_ref[0]).astype(BF16)
    project_rows(first_ref, second_ref, wk, wv_t, key_ref, value_ref, 0)


def project(first, second, block, w_query, w_key, w_value):
    vm = pl.BlockSpec(memory_space=VM)
    return pl.pallas_call(
        project_kernel,
        in_specs=[vm] * 6,
        out_specs=[vm] * 6,
        out_shape=[
            jax.ShapeDtypeStruct((16, TILE, 256), BF16),
            jax.ShapeDtypeStruct((16, 2, VROWS, TILE), BF16),
            jax.ShapeDtypeStruct((4, 2, TILE, PAIR), BF16),
            jax.ShapeDtypeStruct((256, 256), BF16),
            jax.ShapeDtypeStruct((256, TILE), BF16),
            jax.ShapeDtypeStruct((HEADS, TILE), F32),
        ],
        compiler_params=pltpu.CompilerParams(vmem_limit_bytes=8 << 20),
        cost_estimate=pl.CostEstimate(flops=1 << 29, bytes_accessed=4 << 20, transcendentals=0),
        name="project",
    )(first, second, block, w_query, w_key, w_value)


def attend_rows(
    group, spot_list, tile_list, counts, bias_ref, query_ref, key_ref, value_ref, part_ref, acc_ref, score_ref
):
    base = group * STRIDE
    count = counts[group]
    quads = (count + 1) // QUAD
    rest = (count - quads * QUAD + 1) // 2

    def score(start, size, tops):
        tops = list(tops)
        names = [tile_list[base + start + member] for member in range(size)]
        spots = [spot_list[name] for name in names]
        for half in range(2):
            keys = jnp.concatenate([key_ref[spot, :, half * TILE : (half + 1) * TILE] for spot in spots], axis=0)
            scores = jnp.dot(keys, query_ref[group, half], preferred_element_type=F32)
            for member in range(size):
                bias = bias_ref[names[member]].astype(F32)
                part = scores[member * TILE : (member + 1) * TILE] + jnp.concatenate([bias, bias], axis=1)
                score_ref[start + member, half] = part
                tops[half] = jnp.maximum(tops[half], jnp.max(part.reshape(16, 8, PAIR), axis=0))
        return tuple(tops)

    floor = jnp.full((8, PAIR), FLOOR, F32)
    tops = lax.fori_loop(0, quads, lambda trip, tops: score(trip * QUAD, QUAD, tops), (floor, floor))
    tops = lax.fori_loop(0, rest, lambda trip, tops: score(quads * QUAD + trip * 2, 2, tops), tops)
    tops = [jnp.max(top, axis=0, keepdims=True) for top in tops]
    acc_ref[...] = jnp.zeros(acc_ref.shape, F32)

    def mix(start, size):
        spots = [spot_list[tile_list[base + start + member]] for member in range(size)]
        for half in range(2):
            weights = [jnp.exp(score_ref[start + member, half] - tops[half]).astype(BF16) for member in range(size)]
            values = jnp.concatenate([value_ref[spot, half] for spot in spots], axis=1)
            acc_ref[half] += jnp.dot(values, jnp.concatenate(weights, axis=0), preferred_element_type=F32)
        return 0

    lax.fori_loop(0, quads, lambda trip, _: mix(trip * QUAD, QUAD), 0)
    lax.fori_loop(0, rest, lambda trip, _: mix(quads * QUAD + trip * 2, 2), 0)
    for half in range(2):
        acc = acc_ref[half]
        part_ref[pl.ds(half * TILE, 64), :] = acc[:64, :TILE].astype(BF16)
        part_ref[pl.ds(half * TILE + 64, 64), :] = acc[64:TILE, TILE:].astype(BF16)
    spans = [(head // 2, slice((head % 2) * TILE, (head % 2 + 1) * TILE)) for head in range(HEADS)]
    rows = [tops[half][:, lanes] for half, lanes in spans]
    rows += [acc_ref[half, pl.ds(TILE, 1), lanes] for half, lanes in spans]
    left = jnp.concatenate(rows, axis=0)
    pieces = []
    for _ in range(4):
        piece = left.astype(BF16)
        pieces.append(piece)
        left = left - piece.astype(F32)
    part_ref[pl.ds(256, 32), :] = jnp.concatenate(pieces, axis=0)


def join_kernel(first_ref, second_ref, wk_ref, wv_ref, near_keys, near_values, key_ref, value_ref, sem):
    copies = [
        pltpu.make_async_copy(near_keys, key_ref.at[pl.ds(0, 16)], sem.at[0]),
        pltpu.make_async_copy(near_values, value_ref.at[pl.ds(0, 16)], sem.at[1]),
    ]
    for copy in copies:
        copy.start()
    project_rows(first_ref, second_ref, wk_ref[...], wv_ref[...], key_ref, value_ref, 16)
    for copy in copies:
        copy.wait()


def join(first, second, w_key, wv_t, keys, values):
    vm = pl.BlockSpec(memory_space=VM)
    return pl.pallas_call(
        join_kernel,
        in_specs=[vm] * 6,
        out_specs=[vm] * 2,
        out_shape=[
            jax.ShapeDtypeStruct((32, TILE, 256), BF16),
            jax.ShapeDtypeStruct((32, 2, VROWS, TILE), BF16),
        ],
        scratch_shapes=[pltpu.SemaphoreType.DMA((2,))],
        compiler_params=pltpu.CompilerParams(vmem_limit_bytes=4 << 20),
        cost_estimate=pl.CostEstimate(flops=1 << 29, bytes_accessed=4 << 20, transcendentals=0),
        name="join",
    )(first, second, w_key, wv_t, keys, values)


def attend(group, lists, bias, queries, keys, values):
    vm = pl.BlockSpec(memory_space=VM)
    sm = pl.BlockSpec(memory_space=SM)
    return pl.pallas_call(
        functools.partial(attend_rows, group),
        in_specs=[sm] * 3 + [vm] * 4,
        out_specs=vm,
        out_shape=jax.ShapeDtypeStruct((288, TILE), BF16),
        scratch_shapes=[VM((2, VROWS, PAIR), F32), VM((36, 2, TILE, PAIR), F32)],
        compiler_params=pltpu.CompilerParams(vmem_limit_bytes=14 << 20),
        cost_estimate=pl.CostEstimate(flops=1 << 30, bytes_accessed=8 << 20, transcendentals=1 << 20),
    )(*lists, bias, queries, keys, values)


def finish_kernel(part0, part1, part2, part3, tangent_ref, own_ref, self_ref, wo_ref, gain_ref, out_ref):
    parts = (part0, part1, part2, part3)
    tangent = tangent_ref[...]
    vt = own_ref[...].astype(F32)
    stats = []
    for cell in range(4):
        pieces = parts[cell][pl.ds(256, 32), :].astype(F32)
        stats.append(pieces[:8] + pieces[8:16] + pieces[16:24] + pieces[24:])
    mixed = []
    for head in range(HEADS):
        rows = slice(head * 64, head * 64 + 64)
        own = self_ref[pl.ds(head, 1), :]
        tops = [stat[head : head + 1] for stat in stats]
        top = own
        for other in tops:
            top = jnp.maximum(top, other)
        own_exp = jnp.exp(own - top)
        total = own_exp
        weighted = own_exp.astype(BF16).astype(F32) * vt[rows]
        for cell in range(4):
            factor = jnp.exp(tops[cell] - top)
            total += stats[cell][4 + head : 5 + head] * factor
            weighted += parts[cell][pl.ds(head * 64, 64), :].astype(F32) * factor
        mixed.append((weighted / total).astype(BF16))
    mixed = jnp.concatenate(mixed, axis=0)
    shifted = tangent.astype(F32) + lax.dot_general(
        mixed, wo_ref[...], (((0,), (0,)), ((), ())), preferred_element_type=F32
    )
    normed = shifted / jnp.sqrt(jnp.mean(shifted * shifted, axis=-1, keepdims=True) + 1e-06) * gain_ref[...]
    radius = jnp.sqrt(jnp.sum(normed * normed, axis=-1, keepdims=True) + 1e-06)
    ratio = radius / 16.0
    square = ratio * ratio
    series = ratio * (
        1.0 + square / 6.0 * (1.0 + square / 20.0 * (1.0 + square / 42.0 * (1.0 + square / 72.0)))
    )
    plain = 0.5 * (jnp.exp(ratio) - jnp.exp(-ratio))
    stretched = jnp.where(ratio < 0.75, series, plain)
    out_ref[...] = (16.0 * stretched * normed / radius).astype(BF16)


def finish(parts, tangent, own, self_score, w_out, gain):
    vm = pl.BlockSpec(memory_space=VM)
    return pl.pallas_call(
        finish_kernel,
        in_specs=[vm] * 9,
        out_specs=vm,
        out_shape=jax.ShapeDtypeStruct(tangent.shape, BF16),
        compiler_params=pltpu.CompilerParams(vmem_limit_bytes=8 << 20),
        cost_estimate=pl.CostEstimate(flops=1 << 26, bytes_accessed=1 << 20, transcendentals=1 << 12),
        name="finish",
    )(*parts, tangent, own, self_score, w_out, gain)


def swap(value, axis, size, mask):
    return lax.ppermute(value, axis, [(at, at ^ mask) for at in range(size)])


def grow(value, axis, size, mask):
    return jnp.concatenate([value, swap(value, axis, size, mask)], axis=0)


def per_device(points, w_query, w_key, w_value, w_out, gain, cell_counts, tile_slots, edge_masks):
    me_dst = lax.axis_index("dst")
    me_src = lax.axis_index("src")
    meta = jnp.stack([me_dst, me_src, cell_counts[0, 0]]).astype(jnp.int32)
    tangent = log_map(points)
    first, second, block = tangent[:64], tangent[64:], tangent
    for hop, (one, other) in enumerate(((2, 8), (6, 24), (8, 2), (24, 6))):
        new_first = grow(first, "dst", 32, one)
        second = grow(second, "dst", 32, other)
        first = new_first
        if hop < 2:
            block = grow(block, "src", 4, (1, 3)[hop])
            first, second, block = lax.optimization_barrier((first, second, block))
    far_first = swap(first, "dst", 32, 1)
    far_second = swap(second, "dst", 32, 1)
    bias, *lists = prepare(meta, tile_slots[0, 0], edge_masks[0, 0])
    keys, values, queries, wv_t, own, self_score = project(
        first, second, block.reshape(4, TILE, 256), w_query, w_key, w_value
    )
    keys, values = join(far_first, far_second, w_key, wv_t, keys, values)
    parts = []
    for group, mask in ((3, 2), (2, 3), (1, 1), (0, 0)):
        part = attend(group, lists, bias, queries, keys, values)
        if group:
            part = swap(part, "src", 4, mask)
        parts.append(part)
    return finish(parts, tangent, own, self_score, w_out, gain[None, :])


def solution(mesh):
    return jax.shard_map(
        per_device,
        mesh=mesh,
        in_specs=(
            P(("dst", "src"), None),
            P(),
            P(),
            P(),
            P(),
            P(),
            P("dst", "src"),
            P("dst", "src", None),
            P("dst", "src", None, None, None),
        ),
        out_specs=P(("dst", "src"), None),
        check_vma=False,
    )
```

time: 68.4 us -> 63.3 us (0.925)
  blocking collectives: 9.75 us -> 0 us
  starting transfers between devices: 22.6 us -> 25.9 us
  Pallas kernels: 20.1 us -> 21.5 us
    all_to_all x1 -> x0, blocking collectives: 9.75 us -> none  [per_device(): part = lax.all_to_all(part, 'src', 0, 0)]
    ppermute x12 -> x15, starting transfers between devices: 22.6 us -> 25.9 us  [swap(): return lax.ppermute(value, axis, [(at, at ^ mask) for at in range(size)])]
    pallas_call x3 -> x7, Pallas kernels: 18.6 us -> 19.8 us  [the longest x4 13.2 us: attend(): pl.pallas_call(functools.partial(attend_rows, group), in_specs=[sm] * 3 +...]
    ppermute x12 -> x15, waiting for transfers between devices: 10.4 us -> 10.4 us  [swap(): return lax.ppermute(value, axis, [(at, at ^ mask) for at in range(size)])]
  transfers between devices with their start and end apart: 12 -> 15, of which waited for: 4 -> 4; matrix products, arithmetic and copies ran while one was open for 0% -> 0% of each run, Pallas kernels for 6% -> 14%
where the time goes in v1:
time: 63.3 us; the launch traced here: 63.1 us
  starting transfers between devices  25.9 us (41%)
  Pallas kernels  21.5 us (34%)
  waiting for transfers between devices  10.4 us (16%)
  local copies, waits for them, and re-layouts  2.3 us (4%)
  other arithmetic  2.09 us (3%)
  between operations  0.93 us (1%)
    ppermute x15, starting transfers between devices, swap(): return lax.ppermute(value, axis, [(at, at ^ mask) for at in range(size)])  25.9 us
    pallas_call x4, Pallas kernels, attend(): pl.pallas_call(functools.partial(attend_rows, group), in_specs=[sm] * 3 +...  13.2 us
    ppermute x15, waiting for transfers between devices, swap(): return lax.ppermute(value, axis, [(at, at ^ mask) for at in range(size)])  10.4 us
    pallas_call x1, Pallas kernels, prepare(): pl.pallas_call(prep_kernel, in_specs=[sm, sm, pl.BlockSpec(memory_space=p...  3.81 us
    unnamed x17, local copies, waits for them, and re-layouts  2.26 us
    pallas_call x1, Pallas kernels, project(): pl.pallas_call(project_kernel, in_specs=[vm] * 6, out_specs=[vm] * 6, out...  1.68 us
    pallas_call x1, Pallas kernels, join(): pl.pallas_call(join_kernel, in_specs=[vm] * 6, out_specs=[vm] * 2, out_sh...  1.63 us
  transfers between devices with their start and end apart: 15, of which 4 were waited for; matrix products, arithmetic and copies ran while one was open for 0% of the time, Pallas kernels for 14%

profile of v1, /device:TPU:1, one launch (start us, length us, event | category | flops | bytes accessed | tf_op | source)
XLA Modules:
  0.0 63.1 jit_solution(18194462061419867463)
XLA Ops:
  0.0 0.9 %fusion = f32[128]{0:T(128)S(1)} fusion(bf16[128,256]{1,0:T(8,128)(2,1)} %param.9), kind=kLoop, calls=%fused_computation.5 | loop fusion | flops 98176 | bytes 66048 | tf_op jit(solution)/shard_map/reduce_sum | solution.py:33
  1.0 1.0 %fusion.2.tangent_ref = bf16[128,256]{1,0:T(8,128)(2,1)S(1)} fusion(bf16[128,256]{1,0:T(8,128)(2,1)} %param.9, f32[128]{0:T(128)S(1)} %get-tuple-element.44, f32[128]{0:T(128)S(1)} %get-tuple-element.43), kind=kLoop, calls=%fused_computation.7 | loop fusion | flops 131072 | bytes 132096 | tf_op jit(solution)/shard_map/convert_element_type | solution.py:35
  2.0 2.1 %collective-permute-start = (bf16[64,256]{1,0:T(8,128)(2,1)S(1)}, bf16[64,256]{1,0:T(8,128)(2,1)S(1)}, u32[]{:S(2)}, u32[]{:S(2)}) collective-permute-start(bf16[64,256]{1,0:T(8,128)(2,1)S(1)} %get-tuple-element.42), channel_id=1, source_target_pairs={{0,8},{4,12},{8,0},{12,4},{16,24},{20,28},{24,16},{28,20},{32,40},... | collective-permute-start | bytes 98312 | tf_op jit(solution)/shard_map/ppermute | solution.py:329
  4.1 1.6 %collective-permute-start.2 = (bf16[128,256]{1,0:T(8,128)(2,1)S(1)}, bf16[128,256]{1,0:T(8,128)(2,1)S(1)}, u32[]{:S(2)}, u32[]{:S(2)}) collective-permute-start(bf16[128,256]{1,0:T(8,128)(2,1)S(1)} %fusion.2.tangent_ref), channel_id=1, source_target_pairs={{0,1},{1,0},{2,3},{3,2},{4,5},{5,4},{6,7},{7,6},{8,9},{9,8},{10,11... | collective-permute-start | bytes 196616 | tf_op jit(solution)/shard_map/ppermute | solution.py:329
  5.7 1.3 %collective-permute-start.1 = (bf16[64,256]{1,0:T(8,128)(2,1)S(1)}, bf16[64,256]{1,0:T(8,128)(2,1)S(1)}, u32[]{:S(2)}, u32[]{:S(2)}) collective-permute-start(bf16[64,256]{1,0:T(8,128)(2,1)S(1)} %get-tuple-element.41), channel_id=1, source_target_pairs={{0,32},{4,36},{8,40},{12,44},{16,48},{20,52},{24,56},{28,60},{32,0... | collective-permute-start | bytes 98312 | tf_op jit(solution)/shard_map/ppermute | solution.py:329
  7.0 0.0 collective-permute-done
  7.0 1.8 %collective-permute-done.1 = bf16[64,256]{1,0:T(8,128)(2,1)S(1)} collective-permute-done((bf16[64,256]{1,0:T(8,128)(2,1)S(1)}, bf16[64,256]{1,0:T(8,128)(2,1)S(1)}, u32[]{:S(2)}, u32[]{:S(2)}) %collective-permute-start.1) | collective-permute-done | bytes 32800 | tf_op jit(solution)/shard_map/ppermute | solution.py:329
  8.8 0.0 collective-permute-done.2
  8.8 0.0 copy-start.4
  8.8 1.9 %collective-permute-start.3 = (bf16[128,256]{1,0:T(8,128)(2,1)S(1)}, bf16[128,256]{1,0:T(8,128)(2,1)S(1)}, u32[]{:S(2)}, u32[]{:S(2)}) collective-permute-start(bf16[128,256]{1,0:T(8,128)(2,1)S(1)} %pad_maximum_fusion.6), channel_id=1, source_target_pairs={{0,24},{4,28},{8,16},{12,20},{16,8},{20,12},{24,0},{28,4},{32,56},... | collective-permute-start | bytes 196616 | tf_op jit(solution)/shard_map/ppermute | solution.py:329
  10.7 2.5 %collective-permute-start.5 = (bf16[256,256]{1,0:T(8,128)(2,1)S(1)}, bf16[256,256]{1,0:T(8,128)(2,1)S(1)}, u32[]{:S(2)}, u32[]{:S(2)}) collective-permute-start(bf16[256,256]{1,0:T(8,128)(2,1)S(1)} %pad_maximum_fusion.3), channel_id=1, source_target_pairs={{0,3},{1,2},{2,1},{3,0},{4,7},{5,6},{6,5},{7,4},{8,11},{9,10},{10,... | collective-permute-start | bytes 393224 | tf_op jit(solution)/shard_map/ppermute | solution.py:329
  13.2 2.7 %collective-permute-start.4 = (bf16[128,256]{1,0:T(8,128)(2,1)S(1)}, bf16[128,256]{1,0:T(8,128)(2,1)S(1)}, u32[]{:S(2)}, u32[]{:S(2)}) collective-permute-start(bf16[128,256]{1,0:T(8,128)(2,1)S(1)} %pad_maximum_fusion.7), channel_id=1, source_target_pairs={{0,96},{4,100},{8,104},{12,108},{16,112},{20,116},{24,120},{28,124... | collective-permute-start | bytes 196616 | tf_op jit(solution)/shard_map/ppermute | solution.py:329
  15.9 0.0 collective-permute-done.3
  15.9 1.9 %collective-permute-done.4 = bf16[128,256]{1,0:T(8,128)(2,1)S(1)} collective-permute-done((bf16[128,256]{1,0:T(8,128)(2,1)S(1)}, bf16[128,256]{1,0:T(8,128)(2,1)S(1)}, u32[]{:S(2)}, u32[]{:S(2)}) %collective-permute-start.4) | collective-permute-done | bytes 65568 | tf_op jit(solution)/shard_map/ppermute | solution.py:329
  17.8 0.0 collective-permute-done.5
  17.9 0.3 collective-permute-start.8
  18.1 0.0 collective-permute-start.6
  18.2 3.6 %collective-permute-done.8 = bf16[256,256]{1,0:T(8,128)(2,1)S(1)} collective-permute-done((bf16[256,256]{1,0:T(8,128)(2,1)S(1)}, bf16[256,256]{1,0:T(8,128)(2,1)S(1)}, u32[]{:S(2)}, u32[]{:S(2)}) %collective-permute-start.8) | collective-permute-done | bytes 131104 | tf_op jit(solution)/shard_map/ppermute | solution.py:329
  21.8 0.6 %collective-permute-start.9 = (bf16[512,256]{1,0:T(8,128)(2,1)S(1)}, bf16[512,256]{1,0:T(8,128)(2,1)S(1)}, u32[]{:S(2)}, u32[]{:S(2)}) collective-permute-start(bf16[512,256]{1,0:T(8,128)(2,1)S(1)} %pad_maximum_fusion.2), channel_id=1, source_target_pairs={{0,24},{4,28},{8,16},{12,20},{16,8},{20,12},{24,0},{28,4},{32,56},... | collective-permute-start | bytes 786440 | tf_op jit(solution)/shard_map/ppermute | solution.py:329
  22.5 0.0 collective-permute-done.6
  22.5 2.8 %collective-permute-start.7 = (bf16[512,256]{1,0:T(8,128)(2,1)S(1)}, bf16[512,256]{1,0:T(8,128)(2,1)S(1)}, u32[]{:S(2)}, u32[]{:S(2)}) collective-permute-start(bf16[512,256]{1,0:T(8,128)(2,1)S(1)} %pad_maximum_fusion.1), channel_id=1, source_target_pairs={{0,96},{4,100},{8,104},{12,108},{16,112},{20,116},{24,120},{28,124... | collective-permute-start | bytes 786440 | tf_op jit(solution)/shard_map/ppermute | solution.py:329
  25.3 3.1 %collective-permute-done.9 = bf16[512,256]{1,0:T(8,128)(2,1)S(1)} collective-permute-done((bf16[512,256]{1,0:T(8,128)(2,1)S(1)}, bf16[512,256]{1,0:T(8,128)(2,1)S(1)}, u32[]{:S(2)}, u32[]{:S(2)}) %collective-permute-start.9) | collective-permute-done | bytes 262176 | tf_op jit(solution)/shard_map/ppermute | solution.py:329
  28.3 5.6 %collective-permute-start.11 = (bf16[1024,256]{1,0:T(8,128)(2,1)S(1)}, bf16[1024,256]{1,0:T(8,128)(2,1)S(1)}, u32[]{:S(2)}, u32[]{:S(2)}) collective-permute-start(bf16[1024,256]{1,0:T(8,128)(2,1)S(1)} %constant_dynamic-update-slice_fusion.3.second_ref), channel_id=1, source_target_pairs={{0,4},{4,0},{8,12},{12,8},{16,20},{20,16},{24,28},{28,24},{32,36},... | collective-permute-start | bytes 1572872 | tf_op jit(solution)/shard_map/ppermute | solution.py:329
  34.0 0.0 collective-permute-done.7
  34.0 0.0 copy-start.1
  34.0 0.0 copy-start.5
  34.0 0.0 copy-start.6
  34.0 1.2 %collective-permute-start.10 = (bf16[1024,256]{1,0:T(8,128)(2,1)S(1)}, bf16[1024,256]{1,0:T(8,128)(2,1)S(1)}, u32[]{:S(2)}, u32[]{:S(2)}) collective-permute-start(bf16[1024,256]{1,0:T(8,128)(2,1)S(1)} %constant_dynamic-update-slice_fusion.first_ref), channel_id=1, source_target_pairs={{0,4},{4,0},{8,12},{12,8},{16,20},{20,16},{24,28},{28,24},{32,36},... | collective-permute-start | bytes 1572872 | tf_op jit(solution)/shard_map/ppermute | solution.py:329
  35.9 0.1 pad_add_fusion.meta
  35.9 0.0 copy-done.4
  35.9 0.0 copy-start
  35.9 2.2 %copy-done = s32[1,1,64,128,128]{4,3,2,1,0:T(8,128)S(1)} copy-done((s32[1,1,64,128,128]{4,3,2,1,0:T(8,128)S(1)}, s32[1,1,64,128,128]{4,3,2,1,0:T(8,128)}, u32[]{:S(2)}) %copy-start) | copy-done | bytes 4194328
  38.1 3.8 %prep.1 = (bf16[65,128,128]{2,1,0:T(8,128)(2,1)S(1)}, s32[72]{0:T(128)S(1)}, s32[168]{0:T(256)S(1)}, s32[4]{0:T(128)S(1)}) custom-call(s32[3]{0:T(128)S(1)} %pad_add_fusion.meta, s32[64]{0:T(128)S(1)} %bitcast.11, s32[64,128,128]{2,1,0:T(8,128)S(1)} %bitcast.8), custom_call_target="tpu_custom_call" | custom-call | flops 1048576 | bytes 6291456 | tf_op jit(solution)/shard_map/prep/pallas_call | solution.py:91
  41.9 0.0 copy-done.1
  42.0 0.0 copy-done.5
  42.0 0.0 copy-done.6
  42.0 1.7 %project.1 = (bf16[16,128,256]{2,1,0:T(8,128)(2,1)S(1)}, bf16[16,2,144,128]{3,2,1,0:T(8,128)(2,1)S(1)}, bf16[4,2,128,256]{3,2,1,0:T(8,128)(2,1)S(1)}, bf16[256,2...) custom-call(bf16[1024,256]{1,0:T(8,128)(2,1)S(1)} %constant_dynamic-update-slice_fusion.first_ref, ...), custom_call_target="tpu_custom_call" | custom-call | flops 536870912 | bytes 4194304 | tf_op jit(solution)/shard_map/project/pallas_call | solution.py:160
  43.7 0.0 collective-permute-done.11.second_ref
  43.7 0.0 collective-permute-done.10.first_ref
  43.7 1.6 %join.1 = (bf16[32,128,256]{2,1,0:T(8,128)(2,1)S(1)}, bf16[32,2,144,128]{3,2,1,0:T(8,128)(2,1)S(1)}) custom-call(bf16[1024,256]{1,0:T(8,128)(2,1)S(1)} %collective-permute-done.10.first_ref, bf16[1024,256]{1,0:T(8,128)(2,1)S(1)} %collective-permute-done.11.second_ref, bf16[256,256]{1,0:T(8,128)(2,1)S(1)} %copy-done.1, ...), custom_call_target="tpu_custom_call" | custom-call | flops 536870912 | bytes 4194304 | tf_op jit(solution)/shard_map/join/pallas_call | solution.py:246
  45.3 3.1 %shard_map.93 = bf16[288,128]{1,0:T(8,128)(2,1)S(1)} custom-call(s32[72]{0:T(128)S(1)} %get-tuple-element.23.spot_list, s32[168]{0:T(256)S(1)} %get-tuple-element.24.tile_list, s32[4]{0:T(128)S(1)} %get-tuple-element.25.counts, bf16[65,128,128]{2,1,0:T(8,128)(2,1)S(1)} %get-tuple-element.26.bias_ref, ...), custom_call_target="tpu_custom_call" | custom-call | flops 1073741824 | bytes 8388608 | tf_op jit(solution)/shard_map/pallas_call | solution.py:264
  48.4 3.0 %shard_map.92 = bf16[288,128]{1,0:T(8,128)(2,1)S(1)} custom-call(s32[72]{0:T(128)S(1)} %get-tuple-element.23.spot_list, s32[168]{0:T(256)S(1)} %get-tuple-element.24.tile_list, s32[4]{0:T(128)S(1)} %get-tuple-element.25.counts, bf16[65,128,128]{2,1,0:T(8,128)(2,1)S(1)} %get-tuple-element.26.bias_ref, ...), custom_call_target="tpu_custom_call" | custom-call | flops 1073741824 | bytes 8388608 | tf_op jit(solution)/shard_map/pallas_call | solution.py:264
  51.4 3.6 %shard_map.91 = bf16[288,128]{1,0:T(8,128)(2,1)S(1)} custom-call(s32[72]{0:T(128)S(1)} %get-tuple-element.23.spot_list, s32[168]{0:T(256)S(1)} %get-tuple-element.24.tile_list, s32[4]{0:T(128)S(1)} %get-tuple-element.25.counts, bf16[65,128,128]{2,1,0:T(8,128)(2,1)S(1)} %get-tuple-element.26.bias_ref, ...), custom_call_target="tpu_custom_call" | custom-call | flops 1073741824 | bytes 8388608 | tf_op jit(solution)/shard_map/pallas_call | solution.py:264
  55.0 0.0 copy-start.2
  55.0 0.0 copy-start.3
  55.0 0.1 collective-permute-start.14
  55.1 0.1 collective-permute-start.13
  55.2 3.1 %collective-permute-start.12 = (bf16[288,128]{1,0:T(8,128)(2,1)S(1)}, bf16[288,128]{1,0:T(8,128)(2,1)S(1)}, u32[]{:S(2)}, u32[]{:S(2)}) collective-permute-start(bf16[288,128]{1,0:T(8,128)(2,1)S(1)} %shard_map.91), channel_id=1, source_target_pairs={{0,2},{1,3},{2,0},{3,1},{4,6},{5,7},{6,4},{7,5},{8,10},{9,11},{10,... | collective-permute-start | bytes 221192 | tf_op jit(solution)/shard_map/ppermute | solution.py:329
  58.3 3.5 %shard_map.94.part3 = bf16[288,128]{1,0:T(8,128)(2,1)S(1)} custom-call(s32[72]{0:T(128)S(1)} %get-tuple-element.23.spot_list, s32[168]{0:T(256)S(1)} %get-tuple-element.24.tile_list, s32[4]{0:T(128)S(1)} %get-tuple-element.25.counts, bf16[65,128,128]{2,1,0:T(8,128)(2,1)S(1)} %get-tuple-element.26.bias_ref, ...), custom_call_target="tpu_custom_call" | custom-call | flops 1073741824 | bytes 8388608 | tf_op jit(solution)/shard_map/pallas_call | solution.py:264
  61.8 0.0 collective-permute-done.14.part2
  61.9 0.0 collective-permute-done.13.part1
  61.9 0.0 collective-permute-done.12.part0
  61.9 0.0 copy-done.2
  61.9 0.0 copy-done.3
  61.9 1.2 %finish.1 = bf16[128,256]{1,0:T(8,128)(2,1)} custom-call(bf16[288,128]{1,0:T(8,128)(2,1)S(1)} %collective-permute-done.12.part0, bf16[288,128]{1,0:T(8,128)(2,1)S(1)} %collective-permute-done.13.part1, bf16[288,128]{1,0:T(8,128)(2,1)S(1)} %collective-permute-done.14.part2, bf16[288,128]{1,0:T(8,128)(2,1)S(1)} %shard_map.94.part3, ...), custom_call_target="tpu_custom_call" | custom-call | flops 67108864 | bytes 1048576 | tf_op jit(solution)/shard_map/finish/pallas_call | solution.py:317
  (15 shorter events, 0.2 us)
Async XLA Ops:
  2.0 5.0 %collective-permute-start = (bf16[64,256]{1,0:T(8,128)(2,1)S(1)}, bf16[64,256]{1,0:T(8,128)(2,1)S(1)}, u32[]{:S(2)}, u32[]{:S(2)}) collective-permute-start(bf16[64,256]{1,0:T(8,128)(2,1)S(1)} %get-tuple-element.42), channel_id=1, source_target_pairs={{0,8},{4,12},{8,0},{12,4},{16,24},{20,28},{24,16},{28,20},{32,40},... | collective-permute-start | bytes 98312 | tf_op jit(solution)/shard_map/ppermute | solution.py:329
  4.1 4.7 %collective-permute-start.2 = (bf16[128,256]{1,0:T(8,128)(2,1)S(1)}, bf16[128,256]{1,0:T(8,128)(2,1)S(1)}, u32[]{:S(2)}, u32[]{:S(2)}) collective-permute-start(bf16[128,256]{1,0:T(8,128)(2,1)S(1)} %fusion.2.tangent_ref), channel_id=1, source_target_pairs={{0,1},{1,0},{2,3},{3,2},{4,5},{5,4},{6,7},{7,6},{8,9},{9,8},{10,11... | collective-permute-start | bytes 196616 | tf_op jit(solution)/shard_map/ppermute | solution.py:329
  5.7 3.1 %collective-permute-start.1 = (bf16[64,256]{1,0:T(8,128)(2,1)S(1)}, bf16[64,256]{1,0:T(8,128)(2,1)S(1)}, u32[]{:S(2)}, u32[]{:S(2)}) collective-permute-start(bf16[64,256]{1,0:T(8,128)(2,1)S(1)} %get-tuple-element.41), channel_id=1, source_target_pairs={{0,32},{4,36},{8,40},{12,44},{16,48},{20,52},{24,56},{28,60},{32,0... | collective-permute-start | bytes 98312 | tf_op jit(solution)/shard_map/ppermute | solution.py:329
  8.8 27.1 %copy-start.4 = (s32[1,1,64]{2,1,0:T(1,128)S(1)}, s32[1,1,64]{2,1,0:T(1,128)}, u32[]{:S(2)}) copy-start(s32[1,1,64]{2,1,0:T(1,128)} %param.16) | copy-start | bytes 772
  8.8 7.1 %collective-permute-start.3 = (bf16[128,256]{1,0:T(8,128)(2,1)S(1)}, bf16[128,256]{1,0:T(8,128)(2,1)S(1)}, u32[]{:S(2)}, u32[]{:S(2)}) collective-permute-start(bf16[128,256]{1,0:T(8,128)(2,1)S(1)} %pad_maximum_fusion.6), channel_id=1, source_target_pairs={{0,24},{4,28},{8,16},{12,20},{16,8},{20,12},{24,0},{28,4},{32,56},... | collective-permute-start | bytes 196616 | tf_op jit(solution)/shard_map/ppermute | solution.py:329
  10.7 7.2 %collective-permute-start.5 = (bf16[256,256]{1,0:T(8,128)(2,1)S(1)}, bf16[256,256]{1,0:T(8,128)(2,1)S(1)}, u32[]{:S(2)}, u32[]{:S(2)}) collective-permute-start(bf16[256,256]{1,0:T(8,128)(2,1)S(1)} %pad_maximum_fusion.3), channel_id=1, source_target_pairs={{0,3},{1,2},{2,1},{3,0},{4,7},{5,6},{6,5},{7,4},{8,11},{9,10},{10,... | collective-permute-start | bytes 393224 | tf_op jit(solution)/shard_map/ppermute | solution.py:329
  13.2 4.7 %collective-permute-start.4 = (bf16[128,256]{1,0:T(8,128)(2,1)S(1)}, bf16[128,256]{1,0:T(8,128)(2,1)S(1)}, u32[]{:S(2)}, u32[]{:S(2)}) collective-permute-start(bf16[128,256]{1,0:T(8,128)(2,1)S(1)} %pad_maximum_fusion.7), channel_id=1, source_target_pairs={{0,96},{4,100},{8,104},{12,108},{16,112},{20,116},{24,120},{28,124... | collective-permute-start | bytes 196616 | tf_op jit(solution)/shard_map/ppermute | solution.py:329
  17.9 3.9 %collective-permute-start.8 = (bf16[256,256]{1,0:T(8,128)(2,1)S(1)}, bf16[256,256]{1,0:T(8,128)(2,1)S(1)}, u32[]{:S(2)}, u32[]{:S(2)}) collective-permute-start(bf16[256,256]{1,0:T(8,128)(2,1)S(1)} %pad_maximum_fusion.5), channel_id=1, source_target_pairs={{0,8},{4,12},{8,0},{12,4},{16,24},{20,28},{24,16},{28,20},{32,40},... | collective-permute-start | bytes 393224 | tf_op jit(solution)/shard_map/ppermute | solution.py:329
  18.1 4.3 %collective-permute-start.6 = (bf16[256,256]{1,0:T(8,128)(2,1)S(1)}, bf16[256,256]{1,0:T(8,128)(2,1)S(1)}, u32[]{:S(2)}, u32[]{:S(2)}) collective-permute-start(bf16[256,256]{1,0:T(8,128)(2,1)S(1)} %pad_maximum_fusion.4), channel_id=1, source_target_pairs={{0,32},{4,36},{8,40},{12,44},{16,48},{20,52},{24,56},{28,60},{32,0... | collective-permute-start | bytes 393224 | tf_op jit(solution)/shard_map/ppermute | solution.py:329
  21.8 6.5 %collective-permute-start.9 = (bf16[512,256]{1,0:T(8,128)(2,1)S(1)}, bf16[512,256]{1,0:T(8,128)(2,1)S(1)}, u32[]{:S(2)}, u32[]{:S(2)}) collective-permute-start(bf16[512,256]{1,0:T(8,128)(2,1)S(1)} %pad_maximum_fusion.2), channel_id=1, source_target_pairs={{0,24},{4,28},{8,16},{12,20},{16,8},{20,12},{24,0},{28,4},{32,56},... | collective-permute-start | bytes 786440 | tf_op jit(solution)/shard_map/ppermute | solution.py:329
  22.5 11.5 %collective-permute-start.7 = (bf16[512,256]{1,0:T(8,128)(2,1)S(1)}, bf16[512,256]{1,0:T(8,128)(2,1)S(1)}, u32[]{:S(2)}, u32[]{:S(2)}) collective-permute-start(bf16[512,256]{1,0:T(8,128)(2,1)S(1)} %pad_maximum_fusion.1), channel_id=1, source_target_pairs={{0,96},{4,100},{8,104},{12,108},{16,112},{20,116},{24,120},{28,124... | collective-permute-start | bytes 786440 | tf_op jit(solution)/shard_map/ppermute | solution.py:329
  28.3 15.3 %collective-permute-start.11 = (bf16[1024,256]{1,0:T(8,128)(2,1)S(1)}, bf16[1024,256]{1,0:T(8,128)(2,1)S(1)}, u32[]{:S(2)}, u32[]{:S(2)}) collective-permute-start(bf16[1024,256]{1,0:T(8,128)(2,1)S(1)} %constant_dynamic-update-slice_fusion.3.second_ref), channel_id=1, source_target_pairs={{0,4},{4,0},{8,12},{12,8},{16,20},{20,16},{24,28},{28,24},{32,36},... | collective-permute-start | bytes 1572872 | tf_op jit(solution)/shard_map/ppermute | solution.py:329
  34.0 8.0 %copy-start.1 = (bf16[256,256]{1,0:T(8,128)(2,1)S(1)}, bf16[256,256]{1,0:T(8,128)(2,1)}, u32[]{:S(2)}) copy-start(bf16[256,256]{1,0:T(8,128)(2,1)} %wk_ref.3) | copy-start | bytes 393220
  34.0 8.0 %copy-start.5 = (bf16[256,256]{1,0:T(8,128)(2,1)S(1)}, bf16[256,256]{1,0:T(8,128)(2,1)}, u32[]{:S(2)}) copy-start(bf16[256,256]{1,0:T(8,128)(2,1)} %wq_ref.1) | copy-start | bytes 393220
  34.0 8.0 %copy-start.6 = (bf16[256,256]{1,0:T(8,128)(2,1)S(1)}, bf16[256,256]{1,0:T(8,128)(2,1)}, u32[]{:S(2)}) copy-start(bf16[256,256]{1,0:T(8,128)(2,1)} %wv_ref.1) | copy-start | bytes 393220
  34.0 9.7 %collective-permute-start.10 = (bf16[1024,256]{1,0:T(8,128)(2,1)S(1)}, bf16[1024,256]{1,0:T(8,128)(2,1)S(1)}, u32[]{:S(2)}, u32[]{:S(2)}) collective-permute-start(bf16[1024,256]{1,0:T(8,128)(2,1)S(1)} %constant_dynamic-update-slice_fusion.first_ref), channel_id=1, source_target_pairs={{0,4},{4,0},{8,12},{12,8},{16,20},{20,16},{24,28},{28,24},{32,36},... | collective-permute-start | bytes 1572872 | tf_op jit(solution)/shard_map/ppermute | solution.py:329
  35.9 2.2 %copy-start = (s32[1,1,64,128,128]{4,3,2,1,0:T(8,128)S(1)}, s32[1,1,64,128,128]{4,3,2,1,0:T(8,128)}, u32[]{:S(2)}) copy-start(s32[1,1,64,128,128]{4,3,2,1,0:T(8,128)} %param.17) | copy-start | bytes 12582916
  55.0 6.9 %copy-start.2 = (bf16[256,256]{1,0:T(8,128)(2,1)S(1)}, bf16[256,256]{1,0:T(8,128)(2,1)}, u32[]{:S(2)}) copy-start(bf16[256,256]{1,0:T(8,128)(2,1)} %wo_ref.1) | copy-start | bytes 393220
  55.0 6.9 %copy-start.3 = (f32[256]{0:T(256)S(1)}, f32[256]{0:T(256)}, u32[]{:S(2)}) copy-start(f32[256]{0:T(256)} %param.14) | copy-start | bytes 3076
  55.0 6.9 %collective-permute-start.14 = (bf16[288,128]{1,0:T(8,128)(2,1)S(1)}, bf16[288,128]{1,0:T(8,128)(2,1)S(1)}, u32[]{:S(2)}, u32[]{:S(2)}) collective-permute-start(bf16[288,128]{1,0:T(8,128)(2,1)S(1)} %shard_map.93), channel_id=1, source_target_pairs={{0,1},{1,0},{2,3},{3,2},{4,5},{5,4},{6,7},{7,6},{8,9},{9,8},{10,11... | collective-permute-start | bytes 221192 | tf_op jit(solution)/shard_map/ppermute | solution.py:329
  55.1 6.8 %collective-permute-start.13 = (bf16[288,128]{1,0:T(8,128)(2,1)S(1)}, bf16[288,128]{1,0:T(8,128)(2,1)S(1)}, u32[]{:S(2)}, u32[]{:S(2)}) collective-permute-start(bf16[288,128]{1,0:T(8,128)(2,1)S(1)} %shard_map.92), channel_id=1, source_target_pairs={{0,3},{1,2},{2,1},{3,0},{4,7},{5,6},{6,5},{7,4},{8,11},{9,10},{10,... | collective-permute-start | bytes 221192 | tf_op jit(solution)/shard_map/ppermute | solution.py:329
  55.2 6.7 %collective-permute-start.12 = (bf16[288,128]{1,0:T(8,128)(2,1)S(1)}, bf16[288,128]{1,0:T(8,128)(2,1)S(1)}, u32[]{:S(2)}, u32[]{:S(2)}) collective-permute-start(bf16[288,128]{1,0:T(8,128)(2,1)S(1)} %shard_map.91), channel_id=1, source_target_pairs={{0,2},{1,3},{2,0},{3,1},{4,6},{5,7},{6,4},{7,5},{8,10},{9,11},{10,... | collective-permute-start | bytes 221192 | tf_op jit(solution)/shard_map/ppermute | solution.py:329
